TPU v7x, 32 devices: a whole 2x2x4 slice. The times are simulated.
32 devices in a mesh: cache: 2 (over y), tp: 8 (over z, core), cand: 2 (over x).
Axes of the slice: x: 2, y: 2, z: 4, core: 2. Of those that a mesh axis runs over, the one named last changes fastest.
Arguments:
- prompt_inputs: bfloat16 [1536, 8192], P(('cache', 'cand')), may hold values from -6 to 6
- cand_inputs: bfloat16 [4096, 8192], P(('cache', 'cand'), 'tp'), may hold values from -6 to 6
- norm_gain: float32 [8192], replicated, may hold values from 0.1 to 1.9
- w_query: bfloat16 [8192, 8192], P('cache', 'tp'), may hold values from -0.0625 to 0.0625
- w_key: bfloat16 [8192, 1024], P('cache', 'tp'), may hold values from -0.0625 to 0.0625
- w_value: bfloat16 [8192, 1024], P('cache', 'tp'), may hold values from -0.0625 to 0.0625
- q_bias: float32 [8192], P('tp'), may hold values from -180 to 180
- k_bias: float32 [1024], P('tp'), may hold values from -3 to 8
- v_bias: float32 [1024], P('tp'), may hold values from -4 to 4
- cand_lengths: int32 [16], replicated, may hold values from 32 to 256, as said below
- prefix_ends: int32 [16], replicated, may hold values from 384 to 1536, as said below
Outputs:
- attn_out: bfloat16 [4096, 8192], P(('cache', 'cand'), 'tp')
Inputs may be any that keep to these rules, and one draw needn't show every extreme that they name: `cand_lengths`: at least one candidate has 256 tokens. `prefix_ends`: at least one candidate follows the whole prompt.
All inputs are finite; a program needn't handle non-finite values.
Results may differ from a plain program's by a relative error of at most 0.0075.
The roundings to bfloat16 on the way count: a program that leaves them out, or rounds other values in their place, can miss the bound.
Values may be sent and summed in bfloat16 or wider, within the bound.
A program may use at most 192 MiB of HBM per device.

v0:
```python
import jax
import jax.numpy as jnp
from jax import lax
from jax.sharding import PartitionSpec as P

D = 8192
HEADS = 64
KV_HEADS = 8
HEAD = 128
CANDS = 16
CLEN = 256
ROPE_THETA = 1000000.0
EPSILON = 1e-06


def rotate(tensor, positions):
    half_size = tensor.shape[-1] // 2
    inverse_freq = jnp.power(
        ROPE_THETA, -jnp.arange(half_size, dtype=jnp.float32) * 2.0 / tensor.shape[-1]
    )
    angles = positions.astype(jnp.float32)[:, None] * inverse_freq[None, :]
    cosine = jnp.cos(angles)[:, None, :]
    sine_part = jnp.sin(angles)[:, None, :]
    first_half = tensor[..., :half_size]
    second = tensor[..., half_size:]
    return jnp.concatenate(
        [first_half * cosine - second * sine_part, second * cosine + first_half * sine_part],
        axis=-1,
    )


def row_lookup(row_ids, table):
    chosen = (row_ids // CLEN)[:, None] == jnp.arange(CANDS, dtype=jnp.int32)[None, :]
    return jnp.sum(jnp.where(chosen, table[None, :], 0), axis=1)


def key_visible(row_ids, key_index, prefix_row, prompt_dev, cand_dev):
    unit_rows = prompt_dev + cand_dev
    key_owner = key_index // unit_rows
    key_offset = key_index % unit_rows
    is_prompt = key_offset < prompt_dev
    prompt_pos = key_owner * prompt_dev + key_offset
    cand_row = key_owner * cand_dev + key_offset - prompt_dev
    seen_prompt = prompt_pos[None, :] < prefix_row[:, None]
    seen_cand = ((cand_row // CLEN)[None, :] == (row_ids // CLEN)[:, None]) & (
        cand_row[None, :] <= row_ids[:, None]
    )
    return jnp.where(is_prompt[None, :], seen_prompt, seen_cand)


def attend_block(queries, key_rows, value_rows, visible, running):
    maxima, totals, accumulated = running
    scores = jnp.einsum(
        "rgqd,ngd->rgqn", queries, key_rows, preferred_element_type=jnp.float32
    ) * queries.shape[-1] ** (-0.5)
    visible_four = visible[:, None, None, :]
    new_maxima = jnp.maximum(maxima, jnp.max(jnp.where(visible_four, scores, -1e30), axis=-1))
    weights = jnp.exp(jnp.where(visible_four, scores - new_maxima[..., None], -jnp.inf))
    rescale = jnp.exp(maxima - new_maxima)
    totals = totals * rescale + jnp.sum(weights, axis=-1)
    accumulated = accumulated * rescale[..., None] + jnp.einsum(
        "rgqn,ngd->rgqd",
        weights.astype(jnp.bfloat16),
        value_rows,
        preferred_element_type=jnp.float32,
    )
    return (new_maxima, totals, accumulated)


def block_size(total_rows, unit_rows):
    for multiple in (4, 2, 1):
        if total_rows > multiple * unit_rows and total_rows % (multiple * unit_rows) == 0:
            return multiple * unit_rows
    return total_rows


def per_device(
    prompt_inputs,
    cand_inputs,
    norm_gain,
    w_query,
    w_key,
    w_value,
    q_bias,
    k_bias,
    v_bias,
    cand_lengths,
    prefix_ends,
):
    prompt_dev = prompt_inputs.shape[0]
    cand_dev = cand_inputs.shape[0]
    head_size = HEAD
    kv_local = w_key.shape[1] // head_size
    groups = HEADS // KV_HEADS
    kv_width = kv_local * head_size
    joined = lax.axis_index("cache") * lax.axis_size("cand") + lax.axis_index("cand")
    widened_p = prompt_inputs.astype(jnp.float32)
    normed_p = (
        widened_p
        * lax.rsqrt(jnp.mean(widened_p * widened_p, axis=-1, keepdims=True) + EPSILON)
        * norm_gain
    ).astype(jnp.bfloat16)
    widened_c = cand_inputs.astype(jnp.float32)
    squares = lax.psum(jnp.sum(widened_c * widened_c, axis=-1), "tp")
    part_width = cand_inputs.shape[1]
    gain_part = lax.dynamic_slice_in_dim(norm_gain, lax.axis_index("tp") * part_width, part_width)
    normed_part = (widened_c * lax.rsqrt(squares / D + EPSILON)[:, None] * gain_part).astype(
        jnp.bfloat16
    )
    normed_c = lax.all_gather(normed_part, "tp", axis=1, tiled=True)
    row_ids = joined * cand_dev + jnp.arange(cand_dev, dtype=jnp.int32)
    prefix_row = row_lookup(row_ids, prefix_ends)
    length_row = row_lookup(row_ids, cand_lengths)
    cand_pos = prefix_row + row_ids % CLEN
    prompt_pos = joined * prompt_dev + jnp.arange(prompt_dev, dtype=jnp.int32)
    kv_start = (
        jnp.zeros((prompt_dev, 2 * kv_width), jnp.float32),
        jnp.zeros((cand_dev, 2 * kv_width), jnp.float32),
    )
    initial = (kv_start[0], kv_start[1], jnp.zeros((cand_dev, w_query.shape[1]), jnp.float32))
    piece_key = lax.all_gather(w_key, "cache", axis=0, tiled=True)
    piece_value = lax.all_gather(w_value, "cache", axis=0, tiled=True)
    piece_query = lax.all_gather(w_query, "cache", axis=0, tiled=True)
    key_value = jnp.concatenate([piece_key, piece_value], axis=1)
    kv_prompt = jnp.dot(normed_p, key_value, preferred_element_type=jnp.float32)
    kv_cand = jnp.dot(normed_c, key_value, preferred_element_type=jnp.float32)
    q_cand = jnp.dot(normed_c, piece_query, preferred_element_type=jnp.float32)
    keys_p = rotate(
        (kv_prompt[:, :kv_width] + k_bias).reshape(prompt_dev, kv_local, head_size), prompt_pos
    ).astype(jnp.bfloat16)
    values_p = (
        (kv_prompt[:, kv_width:] + v_bias)
        .astype(jnp.bfloat16)
        .reshape(prompt_dev, kv_local, head_size)
    )
    keys_c = rotate(
        (kv_cand[:, :kv_width] + k_bias).reshape(cand_dev, kv_local, head_size), cand_pos
    ).astype(jnp.bfloat16)
    values_c = (
        (kv_cand[:, kv_width:] + v_bias).astype(jnp.bfloat16).reshape(cand_dev, kv_local, head_size)
    )
    queries = rotate(
        (q_cand + q_bias).reshape(cand_dev, kv_local * groups, head_size), cand_pos
    ).astype(jnp.bfloat16)
    queries = queries.reshape(cand_dev, kv_local, groups, head_size)
    keys_all = jnp.concatenate([keys_p, keys_c], axis=0)
    values_all = jnp.concatenate([values_p, values_c], axis=0)
    unit_rows = prompt_dev + cand_dev
    initial = (
        jnp.full((cand_dev, kv_local, groups), -1e30, jnp.float32),
        jnp.zeros((cand_dev, kv_local, groups), jnp.float32),
        jnp.zeros((cand_dev, kv_local, groups, head_size), jnp.float32),
    )
    piece_key = lax.all_gather(keys_all, ("cache", "cand"), axis=0, tiled=True)
    piece_value = lax.all_gather(values_all, ("cache", "cand"), axis=0, tiled=True)
    piece_rows = piece_key.shape[0]
    block_rows = block_size(piece_rows, unit_rows)

    def advance(turn_index, inner):
        first_row = turn_index * block_rows
        key_block = lax.dynamic_slice_in_dim(piece_key, first_row, block_rows, 0)
        value_block = lax.dynamic_slice_in_dim(piece_value, first_row, block_rows, 0)
        key_index = first_row + jnp.arange(block_rows, dtype=jnp.int32)
        visible = key_visible(row_ids, key_index, prefix_row, prompt_dev, cand_dev)
        return attend_block(queries, key_block, value_block, visible, inner)

    maxima, totals, accumulated = lax.fori_loop(0, piece_rows // block_rows, advance, initial)
    result = accumulated / totals[..., None]
    valid_rows = row_ids % CLEN < length_row
    result = jnp.where(valid_rows[:, None, None, None], result, 0.0).astype(jnp.bfloat16)
    return result.reshape(cand_dev, kv_local * groups * head_size)


def solution(mesh):
    placed = (
        P(("cache", "cand"), None),
        P(("cache", "cand"), "tp"),
        P(),
        P("cache", "tp"),
        P("cache", "tp"),
        P("cache", "tp"),
        P("tp"),
        P("tp"),
        P("tp"),
        P(),
        P(),
    )
    return jax.shard_map(
        per_device,
        mesh=mesh,
        in_specs=placed,
        out_specs=P(("cache", "cand"), "tp"),
        check_vma=False,
    )
```

profile of v0, /device:TPU:0, one launch (start us, length us, event | category | flops | bytes accessed | tf_op | source)
XLA Modules:
  0.0 713.0 jit_solution(11202659701899215689)
XLA Ops:
  6.5 0.0 all-gather.7.cloned.1.call-start
  6.5 0.7 all-gather.7.cloned.1.call-update
  7.3 0.0 all-gather.9.cloned.1.call-start
  7.3 0.7 all-gather.9.cloned.1.call-update
  8.0 0.0 all-gather.11.cloned.1.call-start
  8.1 0.7 dynamic_slice.25
  8.8 2.1 fusion.46
  10.8 18.1 %psum.7 = f32[1024]{0:T(1024)S(1)} all-reduce(f32[1024]{0:T(1024)S(1)} %fusion.46), channel_id=1, replica_groups=mesh['cache'=2,'tp'=8,'cand'=2] {'tp'}, use_global_device_ids=true, to_apply=%region_3.4 | all-reduce | flops 1024 | bytes 8192 | tf_op jit(solution)/shard_map/psum | solution.py:104
  28.9 0.0 copy-done
  28.9 1.9 fusion.48
  30.8 0.0 all-gather.11.cloned.1.call-update
  30.8 0.0 copy-start.7
  30.9 0.0 copy-start.8
  30.9 0.0 all-gather.15.cloned.1.call-start
  30.9 0.5 all-gather.15.cloned.1.call-update
  31.4 0.0 all-gather.13.cloned.1.call-start
  31.5 0.0 copy-done.7
  31.6 0.0 copy-done.8
  31.6 0.7 select_reduce_fusion.1
  32.2 4.1 fusion.39
  36.3 0.7 add_convert_fusion.1
  37.0 7.7 %all-gather.7.cloned.1.call-done = bf16[8192,128]{1,0:T(8,128)(2,1)} async-done(((bf16[4096,128]{1,0:T(8,128)(2,1)}), bf16[8192,128]{1,0:T(8,128)(2,1)}) %all-gather.7.cloned.1.call-update) | async-done | bytes 2097168 | tf_op jit(solution)/shard_map/all_gather | solution.py:121
  44.7 3.1 constant_dynamic-update-slice_fusion.1
  47.9 31.5 %all-gather.9.cloned.1.call-done = bf16[8192,128]{1,0:T(8,128)(2,1)} async-done(((bf16[4096,128]{1,0:T(8,128)(2,1)}), bf16[8192,128]{1,0:T(8,128)(2,1)}) %all-gather.9.cloned.1.call-update) | async-done | bytes 2097168 | tf_op jit(solution)/shard_map/all_gather | solution.py:122
  79.4 3.1 constant_dynamic-update-slice_fusion
  82.5 6.6 fusion.42
  89.1 0.0 copy-done.4
  89.1 0.0 copy-done.5
  89.1 0.1 fusion.72
  89.2 0.4 fusion.69
  89.7 142.4 %all-gather.11.cloned.1.call-done = bf16[1024,8192]{1,0:T(8,128)(2,1)} async-done(((bf16[1024,1024]{1,0:T(8,128)(2,1)}), bf16[1024,8192]{1,0:T(8,128)(2,1)}) %all-gather.11.cloned.1.call-update) | async-done | bytes 16777232 | tf_op jit(solution)/shard_map/all_gather | solution.py:110
  232.1 10.6 %fusion.80 = f32[1024,256]{0,1:T(8,128)S(1)} fusion(bf16[1024,8192]{1,0:T(8,128)(2,1)} %all-gather.11.cloned.1.call-done, bf16[8192,256]{1,0:T(8,128)(2,1)} %constant_dynamic-update-slice_fusion), kind=kOutput, calls=%fused_computation.138 | convolution fusion | flops 4294967296 | bytes 22020096 | tf_op jit(solution)/shard_map/dot_general | solution.py:126
  242.7 0.0 copy-start.9
  242.7 0.1 fusion.61
  242.8 1.2 fusion.58
  244.0 0.8 maximum_maximum_fusion
  244.8 0.0 all-gather.13.cloned.1.call-update
  244.8 0.2 all-gather.17.cloned.1.call-start
  245.0 0.6 fusion.78
  245.6 1.9 multiply_cosine_fusion
  247.5 0.8 pad_maximum_fusion.1
  248.3 0.0 all-gather.17.cloned.1.call-update
  248.3 182.3 %all-gather.15.cloned.1.call-done = bf16[8192,1024]{1,0:T(8,128)(2,1)} async-done(((bf16[4096,1024]{1,0:T(8,128)(2,1)}), bf16[8192,1024]{1,0:T(8,128)(2,1)}) %all-gather.15.cloned.1.call-update) | async-done | bytes 16777232 | tf_op jit(solution)/shard_map/all_gather | solution.py:123
  430.6 23.4 %convolution_add_fusion = f32[1024,1024]{0,1:T(8,128)S(1)} fusion(bf16[1024,8192]{1,0:T(8,128)(2,1)} %all-gather.11.cloned.1.call-done, bf16[8192,1024]{1,0:T(8,128)(2,1)} %all-gather.15.cloned.1.call-done, f32[1024]{0:T(1024)S(1)} %copy-done.9), kind=kOutput, calls=%fused_computation.76 | convolution fusion | flops 17180917760 | bytes 37752832 | tf_op jit(solution)/shard_map/dot_general | solution.py:127
  454.0 1.7 fusion.79
  455.7 3.8 copy.30
  459.5 2.7 copy.31
  462.2 4.6 fusion.49
  466.9 2.5 pad_maximum_fusion
  469.3 24.2 %all-gather.17.cloned.1.call-done = bf16[5632,1,128]{0,2,1:T(8,128)(2,1)} async-done(((bf16[1408,1,128]{0,2,1:T(8,128)(2,1)}), bf16[5632,1,128]{0,2,1:T(8,128)(2,1)}) %all-gather.17.cloned.1.call-update) | async-done | bytes 1441808 | tf_op jit(solution)/shard_map/all_gather | solution.py:155
  493.5 207.2 %while.23 = (s32[]{:T(128)}, f32[1024,1,8]{0,2,1:T(8,128)S(1)}, f32[1024,1,8]{0,2,1:T(8,128)}, f32[1024,1,8,128]{0,3,2,1:T(8,128)}, s32[1024]{0:T(1024)}, /*inde...) while((s32[]{:T(128)}, f32[1024,1,8]{0,2,1:T(8,128)S(1)}, ...), condition=%wide.region_8.9_spmd.clone.clone.clone, body=%wide.region_5.8_spmd.clone.clone.clone.sunk | while | flops 12082698240 | bytes 301176576 | solution.py:167
  493.7 5.0 and_select_fusion.2
  498.7 33.8 %fusion.97 = (f32[1024,8]{0,1:T(8,128)S(1)}, f32[2816,1024,8]{1,0,2:T(8,128)}) fusion(pred[1024,2816]{0,1:T(8,128)(4,1)S(1)} %and_select_fusion.2, bf16[1024,1,8,128]{3,0,2,1:T(8,128)(2,1)} %get-tuple-element.550, bf16[5632,1,128]{0,2,1:T(8,128)(2,1)} %get-tuple-element.549, s32[]{:T(128)S(6)} %select_n.299), kind=kOutput, calls=%fused_computation.5.clone.1 | convolution fusion | flops 5974777856 | bytes 98009088 | tf_op jit(solution)/shard_map/while/body/eval_jaxpr/rgqd,ngd->rgqn/dot_general | solution.py:53
  532.5 34.8 %bitcast_add_fusion.5 = f32[1024,1,8,128]{0,3,2,1:T(8,128)} fusion(f32[1024,1,8,128]{0,3,2,1:T(8,128)} %get-tuple-element.534, f32[2816,1024,8]{1,0,2:T(8,128)} %get-tuple-element.516, f32[1024,8]{0,1:T(8,128)S(1)} %bitcast.98, pred[1024,2816]{0,1:T(8,128)(4,1)S(1)} %and_select_fusion.2, f32[1024,8]{0,1:T(8,128)S(1)} %get-tuple-element.517, ...), kind=kOutput, calls=%fused_computation.14.clone.1 | convolution fusion | flops 6001000448 | bytes 104333320 | tf_op jit(solution)/shard_map/while/body/eval_jaxpr/rgqn,ngd->rgqd/dot_general | solution.py:61
  567.3 28.8 %fusion.99 = f32[1024,8]{0,1:T(8,128)S(1)} fusion(f32[2816,1024,8]{1,0,2:T(8,128)} %get-tuple-element.516, f32[1024,8]{0,1:T(8,128)S(1)} %bitcast.99, pred[1024,2816]{0,1:T(8,128)(4,1)S(1)} %and_select_fusion.2), kind=kLoop, calls=%fused_computation.9.clone.1 | loop fusion | flops 92266496 | bytes 95223808 | tf_op jit(solution)/shard_map/while/body/eval_jaxpr/reduce_sum | solution.py:60
  596.2 0.0 copy-start.2
  596.2 0.6 copy-done.2
  597.0 5.0 and_select_fusion.2
  602.0 33.8 %fusion.97 = (f32[1024,8]{0,1:T(8,128)S(1)}, f32[2816,1024,8]{1,0,2:T(8,128)}) fusion(pred[1024,2816]{0,1:T(8,128)(4,1)S(1)} %and_select_fusion.2, bf16[1024,1,8,128]{3,0,2,1:T(8,128)(2,1)} %get-tuple-element.550, bf16[5632,1,128]{0,2,1:T(8,128)(2,1)} %get-tuple-element.549, s32[]{:T(128)S(6)} %select_n.299), kind=kOutput, calls=%fused_computation.5.clone.1 | convolution fusion | flops 5974777856 | bytes 98009088 | tf_op jit(solution)/shard_map/while/body/eval_jaxpr/rgqd,ngd->rgqn/dot_general | solution.py:53
  635.8 35.4 %bitcast_add_fusion.5 = f32[1024,1,8,128]{0,3,2,1:T(8,128)} fusion(f32[1024,1,8,128]{0,3,2,1:T(8,128)} %get-tuple-element.534, f32[2816,1024,8]{1,0,2:T(8,128)} %get-tuple-element.516, f32[1024,8]{0,1:T(8,128)S(1)} %bitcast.98, pred[1024,2816]{0,1:T(8,128)(4,1)S(1)} %and_select_fusion.2, f32[1024,8]{0,1:T(8,128)S(1)} %get-tuple-element.517, ...), kind=kOutput, calls=%fused_computation.14.clone.1 | convolution fusion | flops 6001000448 | bytes 104333320 | tf_op jit(solution)/shard_map/while/body/eval_jaxpr/rgqn,ngd->rgqd/dot_general | solution.py:61
  671.2 28.8 %fusion.99 = f32[1024,8]{0,1:T(8,128)S(1)} fusion(f32[2816,1024,8]{1,0,2:T(8,128)} %get-tuple-element.516, f32[1024,8]{0,1:T(8,128)S(1)} %bitcast.99, pred[1024,2816]{0,1:T(8,128)(4,1)S(1)} %and_select_fusion.2), kind=kLoop, calls=%fused_computation.9.clone.1 | loop fusion | flops 92266496 | bytes 95223808 | tf_op jit(solution)/shard_map/while/body/eval_jaxpr/reduce_sum | solution.py:60
  700.1 0.6 copy-done.2
  700.7 2.8 select_convert_fusion
  703.6 2.6 copy.28
  (40 shorter events, 0.4 us)
Async XLA Ops:
  6.5 22.4 %copy-start = (bf16[1024,1024]{1,0:T(8,128)(2,1)S(1)}, bf16[1024,1024]{1,0:T(8,128)(2,1)}, u32[]{:S(2)}) copy-start(bf16[1024,1024]{1,0:T(8,128)(2,1)} %param.14) | copy-start | bytes 6291460
  6.5 38.2 %all-gather.7.cloned.1.call-start = ((), (), s32[]{:S(2)}) async-start(), calls=%async_computation | async-start | bytes 3145728 | tf_op jit(solution)/shard_map/all_gather | solution.py:121
  7.3 72.1 %all-gather.9.cloned.1.call-start = ((), (), s32[]{:S(2)}) async-start(), calls=%async_computation.1 | async-start | bytes 3145728 | tf_op jit(solution)/shard_map/all_gather | solution.py:122
  8.0 224.1 %all-gather.11.cloned.1.call-start = ((), (), s32[]{:S(2)}) async-start(), calls=%async_computation.2 | async-start | bytes 18874368 | tf_op jit(solution)/shard_map/all_gather | solution.py:110
  30.8 0.7 copy-start.7
  30.9 0.7 copy-start.8
  30.9 399.7 %all-gather.15.cloned.1.call-start = ((), (), s32[]{:S(2)}) async-start(), calls=%async_computation.4 | async-start | bytes 25165824 | tf_op jit(solution)/shard_map/all_gather | solution.py:123
  31.4 437.9 %all-gather.13.cloned.1.call-start = ((), (), s32[]{:S(2)}) async-start(), calls=%async_computation.3 | async-start | bytes 1802240 | tf_op jit(solution)/shard_map/all_gather | solution.py:154
  37.0 45.4 %copy-start.6 = (f32[8192]{0:T(1024)S(1)}, f32[8192]{0:T(1024)}, u32[]{:S(2)}) copy-start(f32[8192]{0:T(1024)} %param.15) | copy-start | bytes 98308
  82.5 6.6 copy-start.4
  82.5 6.6 copy-start.5
  242.7 187.9 %copy-start.9 = (f32[1024]{0:T(1024)S(1)}, f32[1024]{0:T(1024)}, u32[]{:S(2)}) copy-start(f32[1024]{0:T(1024)} %param.19) | copy-start | bytes 12292
  244.8 248.8 %all-gather.17.cloned.1.call-start = ((), (), s32[]{:S(2)}) async-start(), calls=%async_computation.5 | async-start | bytes 1802240 | tf_op jit(solution)/shard_map/all_gather | solution.py:155
  493.5 207.2 %copy-start.3 = (pred[1024]{0:T(1024)(128)(4,1)S(1)}, pred[1024]{0:T(1024)(128)(4,1)}, u32[]{:S(2)}) copy-start(pred[1024]{0:T(1024)(128)(4,1)} %fusion.78) | copy-start | bytes 3076
  567.3 28.9 %copy-start.1 = (f32[1024,1,8]{0,2,1:T(8,128)S(1)}, f32[1024,1,8]{0,2,1:T(8,128)}, u32[]{:S(2)}) copy-start(f32[1024,1,8]{0,2,1:T(8,128)} %get-tuple-element.533) | copy-start | bytes 98308 | tf_op jit(solution)/shard_map/while
  596.2 0.6 copy-start.2
  671.2 28.9 %copy-start.1 = (f32[1024,1,8]{0,2,1:T(8,128)S(1)}, f32[1024,1,8]{0,2,1:T(8,128)}, u32[]{:S(2)}) copy-start(f32[1024,1,8]{0,2,1:T(8,128)} %get-tuple-element.533) | copy-start | bytes 98308 | tf_op jit(solution)/shard_map/while
  700.1 0.6 copy-start.2
Sparse Core Ops, SparseCore 0:
  8.9 35.8 all-gather.6
  46.3 33.0 all-gather.8
  81.0 151.0 all-gather.10
  233.5 197.0 all-gather.14
  432.3 29.7 all-gather.12
  463.7 29.7 all-gather.16
where the time goes:
time: 714 us; the launch traced here: 713 us
  waiting for transfers between devices  390 us (55%)
  matrix products  178 us (25%)
  other arithmetic  93.2 us (13%)
  local copies, waits for them, and re-layouts  18.9 us (3%)
  blocking collectives  18.1 us (3%)
  between operations  13.7 us (2%)
    all_gather x1, waiting for transfers between devices, per_device(): piece_query = lax.all_gather(w_query, 'cache', axis=0, tiled=True)  182 us
    all_gather x1, waiting for transfers between devices, per_device(): normed_c = lax.all_gather(normed_part, 'tp', axis=1, tiled=True)  142 us
    dot_general x2, matrix products, attend_block(): jnp.einsum('rgqn,ngd->rgqd', weights.astype(jnp.bfloat16), value_rows, pr...  70.2 us
    dot_general x2, matrix products, attend_block(): jnp.einsum('rgqd,ngd->rgqn', queries, key_rows, preferred_element_type=jn...  67.6 us
    reduce_sum x2, other arithmetic, attend_block(): totals = totals * rescale + jnp.sum(weights, axis=-1)  57.7 us
    all_gather x1, waiting for transfers between devices, per_device(): piece_value = lax.all_gather(w_value, 'cache', axis=0, tiled=True)  31.5 us
    all_gather x1, waiting for transfers between devices, per_device(): lax.all_gather(values_all, ('cache', 'cand'), axis=0, tiled=True)  24.2 us
    dot_general x1, matrix products, per_device(): q_cand = jnp.dot(normed_c, piece_query, preferred_element_type=jnp.float32)  23.4 us
  transfers between devices with their start and end apart: 6, of which 5 were waited for; matrix products, arithmetic and copies ran while one was open for 11% of the time, Pallas kernels for 0%

commit v1 on v0

--- a/solution.py
+++ b/solution.py
@@ -107,7 +107,12 @@
     normed_part = (widened_c * lax.rsqrt(squares / D + EPSILON)[:, None] * gain_part).astype(
         jnp.bfloat16
     )
-    normed_c = lax.all_gather(normed_part, "tp", axis=1, tiled=True)
+    ring = [normed_part]
+    for hop in range(7):
+        ring.append(lax.ppermute(ring[-1], "tp", [(dev, (dev + 1) % 8) for dev in range(8)]))
+    normed_c = jnp.roll(
+        jnp.concatenate(ring[::-1], axis=1), (lax.axis_index("tp") + 1) * ring[0].shape[1], axis=1
+    )
     row_ids = joined * cand_dev + jnp.arange(cand_dev, dtype=jnp.int32)
     prefix_row = row_lookup(row_ids, prefix_ends)
     length_row = row_lookup(row_ids, cand_lengths)

time: 714 us -> 563 us (0.79)
  waiting for transfers between devices: 390 us -> 198 us
  local copies, waits for them, and re-layouts: 18.9 us -> 58.6 us
    all_gather x1, waiting for transfers between devices: 182 us -> 0.02 us  [per_device(): piece_query = lax.all_gather(w_query, 'cache', axis=0, tiled=True)]
    ppermute x0 -> x7, waiting for transfers between devices: none -> 175 us  [per_device(): lax.ppermute(ring[-1], 'tp', [(dev, (dev + 1) % 8) for dev in range(8)])]
    all_gather x1 -> x0, waiting for transfers between devices: 142 us -> none  [per_device(): normed_c = lax.all_gather(normed_part, 'tp', axis=1, tiled=True)]
    unnamed x19 -> x43, local copies, waits for them, and re-layouts: 9.71 us -> 49.3 us
    all_gather x1, waiting for transfers between devices: 31.5 us -> 0.01 us  [per_device(): piece_value = lax.all_gather(w_value, 'cache', axis=0, tiled=True)]
    all_gather x1, waiting for transfers between devices: 24.2 us -> 0.01 us  [per_device(): lax.all_gather(values_all, ('cache', 'cand'), axis=0, tiled=True)]
    all_gather x1, waiting for transfers between devices: 0.01 us -> 22.3 us  [per_device(): piece_key = lax.all_gather(keys_all, ('cache', 'cand'), axis=0, tiled=True)]
    all_gather x1, waiting for transfers between devices: 7.69 us -> 0.01 us  [per_device(): piece_key = lax.all_gather(w_key, 'cache', axis=0, tiled=True)]
  transfers between devices with their start and end apart: 6 -> 12, of which waited for: 5 -> 8; matrix products, arithmetic and copies ran while one was open for 11% -> 21% of each run, Pallas kernels for 0% -> 0%
where the time goes in v1:
time: 563 us; the launch traced here: 562 us
  waiting for transfers between devices  198 us (35%)
  matrix products  176 us (31%)
  other arithmetic  96.9 us (17%)
  local copies, waits for them, and re-layouts  58.6 us (10%)
  blocking collectives  18.1 us (3%)
  between operations  13.4 us (2%)
    ppermute x7, waiting for transfers between devices, per_device(): lax.ppermute(ring[-1], 'tp', [(dev, (dev + 1) % 8) for dev in range(8)])  175 us
    dot_general x2, matrix products, attend_block(): jnp.einsum('rgqn,ngd->rgqd', weights.astype(jnp.bfloat16), value_rows, pr...  70.1 us
    dot_general x2, matrix products, attend_block(): jnp.einsum('rgqd,ngd->rgqn', queries, key_rows, preferred_element_type=jn...  67.6 us
    reduce_sum x2, other arithmetic, attend_block(): totals = totals * rescale + jnp.sum(weights, axis=-1)  57.7 us
    unnamed x43, local copies, waits for them, and re-layouts  49.3 us
    dot_general x1, matrix products, per_device(): q_cand = jnp.dot(normed_c, piece_query, preferred_element_type=jnp.float32)  23.4 us
    all_gather x1, waiting for transfers between devices, per_device(): piece_key = lax.all_gather(keys_all, ('cache', 'cand'), axis=0, tiled=True)  22.3 us
    psum x1, blocking collectives, per_device(): squares = lax.psum(jnp.sum(widened_c * widened_c, axis=-1), 'tp')  18.1 us
  transfers between devices with their start and end apart: 12, of which 8 were waited for; matrix products, arithmetic and copies ran while one was open for 21% of the time, Pallas kernels for 0%

profile of v1, /device:TPU:0, one launch (start us, length us, event | category | flops | bytes accessed | tf_op | source)
XLA Modules:
  0.0 561.8 jit_solution(13245609389651759619)
XLA Ops:
  6.5 0.7 all-gather.6.cloned.1.call-update
  7.3 0.7 dynamic_slice.29
  8.0 2.1 fusion.50
  10.1 18.1 %psum.7 = f32[1024]{0:T(1024)S(1)} all-reduce(f32[1024]{0:T(1024)S(1)} %fusion.50), channel_id=1, replica_groups=mesh['cache'=2,'tp'=8,'cand'=2] {'tp'}, use_global_device_ids=true, to_apply=%region_3.4 | all-reduce | flops 1024 | bytes 8192 | tf_op jit(solution)/shard_map/psum | solution.py:104
  28.2 1.9 fusion.52
  30.1 27.5 %collective-permute-done = bf16[1024,1024]{1,0:T(8,128)(2,1)} collective-permute-done((bf16[1024,1024]{1,0:T(8,128)(2,1)}, bf16[1024,1024]{1,0:T(8,128)(2,1)}, u32[]{:S(2)}, u32[]{:S(2)}) %collective-permute-start) | collective-permute-done | bytes 2097184 | tf_op jit(solution)/shard_map/ppermute | solution.py:112
  57.7 27.5 %collective-permute-done.1 = bf16[1024,1024]{1,0:T(8,128)(2,1)} collective-permute-done((bf16[1024,1024]{1,0:T(8,128)(2,1)}, bf16[1024,1024]{1,0:T(8,128)(2,1)}, u32[]{:S(2)}, u32[]{:S(2)}) %collective-permute-start.1) | collective-permute-done | bytes 2097184 | tf_op jit(solution)/shard_map/ppermute | solution.py:112
  85.2 27.5 %collective-permute-done.2 = bf16[1024,1024]{1,0:T(8,128)(2,1)S(1)} collective-permute-done((bf16[1024,1024]{1,0:T(8,128)(2,1)}, bf16[1024,1024]{1,0:T(8,128)(2,1)S(1)}, u32[]{:S(2)}, u32[]{:S(2)}) %collective-permute-start.2) | collective-permute-done | bytes 2097184 | tf_op jit(solution)/shard_map/ppermute | solution.py:112
  112.7 1.3 copy-done.1
  114.0 27.3 %collective-permute-done.3 = bf16[1024,1024]{1,0:T(8,128)(2,1)S(1)} collective-permute-done((bf16[1024,1024]{1,0:T(8,128)(2,1)S(1)}, bf16[1024,1024]{1,0:T(8,128)(2,1)S(1)}, u32[]{:S(2)}, u32[]{:S(2)}) %collective-permute-start.3) | collective-permute-done | bytes 2097184 | tf_op jit(solution)/shard_map/ppermute | solution.py:112
  141.3 1.3 copy-done.3
  142.6 27.4 %collective-permute-done.4 = bf16[1024,1024]{1,0:T(8,128)(2,1)} collective-permute-done((bf16[1024,1024]{1,0:T(8,128)(2,1)S(1)}, bf16[1024,1024]{1,0:T(8,128)(2,1)}, u32[]{:S(2)}, u32[]{:S(2)}) %collective-permute-start.4) | collective-permute-done | bytes 2097184 | tf_op jit(solution)/shard_map/ppermute | solution.py:112
  169.9 4.1 fusion.43
  174.1 23.4 %collective-permute-done.5 = bf16[1024,1024]{1,0:T(8,128)(2,1)} collective-permute-done((bf16[1024,1024]{1,0:T(8,128)(2,1)}, bf16[1024,1024]{1,0:T(8,128)(2,1)}, u32[]{:S(2)}, u32[]{:S(2)}) %collective-permute-start.5) | collective-permute-done | bytes 2097184 | tf_op jit(solution)/shard_map/ppermute | solution.py:112
  197.5 3.1 constant_dynamic-update-slice_fusion.1
  200.6 3.2 constant_dynamic-update-slice_fusion
  203.7 6.6 %fusion.46 = f32[384,256]{0,1:T(8,128)S(1)} fusion(bf16[8192,256]{1,0:T(8,128)(2,1)} %constant_dynamic-update-slice_fusion, bf16[384,8192]{1,0:T(8,128)(2,1)} %param.13, f32[8192]{0:T(1024)S(1)} %copy-done.11, f32[384]{0:T(512)S(1)} %add_rsqrt_fusion.1), kind=kOutput, calls=%fused_computation.69 | convolution fusion | flops 1623195648 | bytes 10913280 | tf_op jit(solution)/shard_map/dot_general | solution.py:130
  210.5 14.6 %collective-permute-done.6 = bf16[1024,1024]{1,0:T(8,128)(2,1)} collective-permute-done((bf16[1024,1024]{1,0:T(8,128)(2,1)}, bf16[1024,1024]{1,0:T(8,128)(2,1)}, u32[]{:S(2)}, u32[]{:S(2)}) %collective-permute-start.6) | collective-permute-done | bytes 2097184 | tf_op jit(solution)/shard_map/ppermute | solution.py:112
  225.1 3.1 constant_dynamic-update-slice_fusion.17
  228.1 3.2 constant_dynamic-update-slice_fusion.16
  231.3 3.2 constant_dynamic-update-slice_fusion.15
  234.6 1.5 constant_dynamic-update-slice_fusion.14
  236.0 1.5 constant_dynamic-update-slice_fusion.13
  237.5 3.1 constant_dynamic-update-slice_fusion.12
  240.6 3.1 constant_dynamic-update-slice_fusion.11
  243.7 1.8 constant_dynamic-update-slice_fusion.10
  245.5 3.1 constant_dynamic-update-slice_fusion.9
  248.6 3.0 constant_dynamic-update-slice_fusion.8
  251.6 3.0 constant_dynamic-update-slice_fusion.7
  254.7 1.5 constant_dynamic-update-slice_fusion.6
  256.2 1.5 constant_dynamic-update-slice_fusion.5
  257.7 3.1 constant_dynamic-update-slice_fusion.4
  260.7 3.2 constant_dynamic-update-slice_fusion.3
  263.9 1.9 constant_dynamic-update-slice_fusion.2
  265.8 8.3 %fusion.41 = f32[1024,256]{0,1:T(8,128)S(1)} fusion(bf16[8192,256]{1,0:T(8,128)(2,1)S(1)} %copy-done.7, bf16[1024,16384]{1,0:T(8,128)(2,1)} %constant_dynamic-update-slice_fusion.2, s32[]{:T(128)S(6)} %select_n.221), kind=kOutput, calls=%fused_computation.64 | convolution fusion | flops 4294967296 | bytes 22020100 | tf_op jit(solution)/shard_map/dot_general | solution.py:131
  274.2 0.8 pad_maximum_fusion.1
  275.0 0.3 all-gather.10.cloned.1.call-start
  275.4 0.7 select_reduce_fusion.1
  276.1 0.5 fusion.85
  276.6 0.7 add_convert_fusion.1
  277.3 1.9 multiply_cosine_fusion
  279.2 0.5 fusion.76
  279.7 1.2 fusion.65
  280.8 0.8 maximum_maximum_fusion
  281.7 23.4 %fusion.53 = f32[1024,1024]{0,1:T(8,128)S(1)} fusion(bf16[8192,1024]{1,0:T(8,128)(2,1)} %all-gather.12.cloned.1.call-done, bf16[1024,16384]{1,0:T(8,128)(2,1)} %constant_dynamic-update-slice_fusion.2, s32[]{:T(128)S(6)} %select_n.221, f32[1024]{0:T(1024)S(1)} %copy-done.14), kind=kOutput, calls=%fused_computation.80 | convolution fusion | flops 17180917760 | bytes 37752836 | tf_op jit(solution)/shard_map/dot_general | solution.py:132
  305.1 1.7 fusion.88
  306.8 3.9 copy.30
  310.7 2.7 copy.31
  313.4 4.6 fusion.56
  318.0 2.5 pad_maximum_fusion
  320.5 22.3 %all-gather.10.cloned.1.call-done = bf16[5632,1,128]{0,2,1:T(8,128)(2,1)} async-done(((bf16[1408,1,128]{0,2,1:T(8,128)(2,1)}), bf16[5632,1,128]{0,2,1:T(8,128)(2,1)}) %all-gather.10.cloned.1.call-update) | async-done | bytes 1441808 | tf_op jit(solution)/shard_map/all_gather | solution.py:159
  342.8 207.1 %while.23 = (s32[]{:T(128)}, f32[1024,1,8]{0,2,1:T(8,128)S(1)}, f32[1024,1,8]{0,2,1:T(8,128)}, f32[1024,1,8,128]{0,3,2,1:T(8,128)}, s32[1024]{0:T(1024)}, /*inde...) while((s32[]{:T(128)}, f32[1024,1,8]{0,2,1:T(8,128)S(1)}, ...), condition=%wide.region_8.9_spmd.clone.clone.clone, body=%wide.region_5.8_spmd.clone.clone.clone.sunk | while | flops 12082698240 | bytes 301176576 | solution.py:172
  342.9 5.0 and_select_fusion.2
  348.0 33.8 %fusion.103 = (f32[1024,8]{0,1:T(8,128)S(1)}, f32[2816,1024,8]{1,0,2:T(8,128)}) fusion(pred[1024,2816]{0,1:T(8,128)(4,1)S(1)} %and_select_fusion.2, bf16[1024,1,8,128]{3,0,2,1:T(8,128)(2,1)} %get-tuple-element.550, bf16[5632,1,128]{0,2,1:T(8,128)(2,1)} %get-tuple-element.549, s32[]{:T(128)S(6)} %select_n.313), kind=kOutput, calls=%fused_computation.5.clone.1 | convolution fusion | flops 5974777856 | bytes 98009088 | tf_op jit(solution)/shard_map/while/body/eval_jaxpr/rgqd,ngd->rgqn/dot_general | solution.py:53
  381.8 34.7 %bitcast_add_fusion.5 = f32[1024,1,8,128]{0,3,2,1:T(8,128)} fusion(f32[1024,1,8,128]{0,3,2,1:T(8,128)} %get-tuple-element.534, f32[2816,1024,8]{1,0,2:T(8,128)} %get-tuple-element.516, f32[1024,8]{0,1:T(8,128)S(1)} %bitcast.96, pred[1024,2816]{0,1:T(8,128)(4,1)S(1)} %and_select_fusion.2, f32[1024,8]{0,1:T(8,128)S(1)} %get-tuple-element.517, ...), kind=kOutput, calls=%fused_computation.14.clone.1 | convolution fusion | flops 6001000448 | bytes 104333320 | tf_op jit(solution)/shard_map/while/body/eval_jaxpr/rgqn,ngd->rgqd/dot_general | solution.py:61
  416.5 28.8 %fusion.105 = f32[1024,8]{0,1:T(8,128)S(1)} fusion(f32[2816,1024,8]{1,0,2:T(8,128)} %get-tuple-element.516, f32[1024,8]{0,1:T(8,128)S(1)} %bitcast.97, pred[1024,2816]{0,1:T(8,128)(4,1)S(1)} %and_select_fusion.2), kind=kLoop, calls=%fused_computation.9.clone.1 | loop fusion | flops 92266496 | bytes 95223808 | tf_op jit(solution)/shard_map/while/body/eval_jaxpr/reduce_sum | solution.py:60
  445.4 0.6 copy-done.6
  446.1 5.0 and_select_fusion.2
  451.2 33.8 %fusion.103 = (f32[1024,8]{0,1:T(8,128)S(1)}, f32[2816,1024,8]{1,0,2:T(8,128)}) fusion(pred[1024,2816]{0,1:T(8,128)(4,1)S(1)} %and_select_fusion.2, bf16[1024,1,8,128]{3,0,2,1:T(8,128)(2,1)} %get-tuple-element.550, bf16[5632,1,128]{0,2,1:T(8,128)(2,1)} %get-tuple-element.549, s32[]{:T(128)S(6)} %select_n.313), kind=kOutput, calls=%fused_computation.5.clone.1 | convolution fusion | flops 5974777856 | bytes 98009088 | tf_op jit(solution)/shard_map/while/body/eval_jaxpr/rgqd,ngd->rgqn/dot_general | solution.py:53
  485.0 35.4 %bitcast_add_fusion.5 = f32[1024,1,8,128]{0,3,2,1:T(8,128)} fusion(f32[1024,1,8,128]{0,3,2,1:T(8,128)} %get-tuple-element.534, f32[2816,1024,8]{1,0,2:T(8,128)} %get-tuple-element.516, f32[1024,8]{0,1:T(8,128)S(1)} %bitcast.96, pred[1024,2816]{0,1:T(8,128)(4,1)S(1)} %and_select_fusion.2, f32[1024,8]{0,1:T(8,128)S(1)} %get-tuple-element.517, ...), kind=kOutput, calls=%fused_computation.14.clone.1 | convolution fusion | flops 6001000448 | bytes 104333320 | tf_op jit(solution)/shard_map/while/body/eval_jaxpr/rgqn,ngd->rgqd/dot_general | solution.py:61
  520.4 28.8 %fusion.105 = f32[1024,8]{0,1:T(8,128)S(1)} fusion(f32[2816,1024,8]{1,0,2:T(8,128)} %get-tuple-element.516, f32[1024,8]{0,1:T(8,128)S(1)} %bitcast.97, pred[1024,2816]{0,1:T(8,128)(4,1)S(1)} %and_select_fusion.2), kind=kLoop, calls=%fused_computation.9.clone.1 | loop fusion | flops 92266496 | bytes 95223808 | tf_op jit(solution)/shard_map/while/body/eval_jaxpr/reduce_sum | solution.py:60
  549.3 0.6 copy-done.6
  549.9 2.8 select_convert_fusion
  552.7 2.6 copy.28
  (77 shorter events, 0.9 us)
Async XLA Ops:
  6.5 21.7 %copy-start = (bf16[1024,1024]{1,0:T(8,128)(2,1)S(1)}, bf16[1024,1024]{1,0:T(8,128)(2,1)}, u32[]{:S(2)}) copy-start(bf16[1024,1024]{1,0:T(8,128)(2,1)} %param.14) | copy-start | bytes 6291460
  6.5 191.0 %all-gather.6.cloned.1.call-start = ((), (), s32[]{:S(2)}) async-start(), calls=%async_computation | async-start | bytes 3145728 | tf_op jit(solution)/shard_map/all_gather | solution.py:126
  7.3 193.3 %all-gather.8.cloned.1.call-start = ((), (), s32[]{:S(2)}) async-start(), calls=%async_computation.1 | async-start | bytes 3145728 | tf_op jit(solution)/shard_map/all_gather | solution.py:127
  30.1 27.6 %collective-permute-start = (bf16[1024,1024]{1,0:T(8,128)(2,1)}, bf16[1024,1024]{1,0:T(8,128)(2,1)}, u32[]{:S(2)}, u32[]{:S(2)}) collective-permute-start(bf16[1024,1024]{1,0:T(8,128)(2,1)} %fusion.52), channel_id=1, source_target_pairs={{0,2},{2,4},{4,6},{6,8},{8,10},{10,12},{12,14},{14,0},{1,3},{3,5},... | collective-permute-start | bytes 6291464 | tf_op jit(solution)/shard_map/ppermute | solution.py:112
  30.1 251.6 %all-gather.12.cloned.1.call-start = ((), (), s32[]{:S(2)}) async-start(), calls=%async_computation.3 | async-start | bytes 25165824 | tf_op jit(solution)/shard_map/all_gather | solution.py:128
  57.6 27.6 %collective-permute-start.1 = (bf16[1024,1024]{1,0:T(8,128)(2,1)}, bf16[1024,1024]{1,0:T(8,128)(2,1)}, u32[]{:S(2)}, u32[]{:S(2)}) collective-permute-start(bf16[1024,1024]{1,0:T(8,128)(2,1)} %collective-permute-done), channel_id=1, source_target_pairs={{0,2},{2,4},{4,6},{6,8},{8,10},{10,12},{12,14},{14,0},{1,3},{3,5},... | collective-permute-start | bytes 6291464 | tf_op jit(solution)/shard_map/ppermute | solution.py:112
  57.7 262.8 %all-gather.14.cloned.1.call-start = ((), (), s32[]{:S(2)}) async-start(), calls=%async_computation.4 | async-start | bytes 1802240 | tf_op jit(solution)/shard_map/all_gather | solution.py:160
  85.2 27.5 %collective-permute-start.2 = (bf16[1024,1024]{1,0:T(8,128)(2,1)}, bf16[1024,1024]{1,0:T(8,128)(2,1)S(1)}, u32[]{:S(2)}, u32[]{:S(2)}) collective-permute-start(bf16[1024,1024]{1,0:T(8,128)(2,1)} %collective-permute-done.1), channel_id=1, source_target_pairs={{0,2},{2,4},{4,6},{6,8},{8,10},{10,12},{12,14},{14,0},{1,3},{3,5},... | collective-permute-start | bytes 6291464 | tf_op jit(solution)/shard_map/ppermute | solution.py:112
  112.7 1.3 copy-start.1
  114.0 27.3 %collective-permute-start.3 = (bf16[1024,1024]{1,0:T(8,128)(2,1)S(1)}, bf16[1024,1024]{1,0:T(8,128)(2,1)S(1)}, u32[]{:S(2)}, u32[]{:S(2)}) collective-permute-start(bf16[1024,1024]{1,0:T(8,128)(2,1)S(1)} %collective-permute-done.2), channel_id=1, source_target_pairs={{0,2},{2,4},{4,6},{6,8},{8,10},{10,12},{12,14},{14,0},{1,3},{3,5},... | collective-permute-start | bytes 6291464 | tf_op jit(solution)/shard_map/ppermute | solution.py:112
  141.3 1.3 copy-start.3
  142.6 27.4 %collective-permute-start.4 = (bf16[1024,1024]{1,0:T(8,128)(2,1)S(1)}, bf16[1024,1024]{1,0:T(8,128)(2,1)}, u32[]{:S(2)}, u32[]{:S(2)}) collective-permute-start(bf16[1024,1024]{1,0:T(8,128)(2,1)S(1)} %collective-permute-done.3), channel_id=1, source_target_pairs={{0,2},{2,4},{4,6},{6,8},{8,10},{10,12},{12,14},{14,0},{1,3},{3,5},... | collective-permute-start | bytes 6291464 | tf_op jit(solution)/shard_map/ppermute | solution.py:112
  169.9 27.6 %collective-permute-start.5 = (bf16[1024,1024]{1,0:T(8,128)(2,1)}, bf16[1024,1024]{1,0:T(8,128)(2,1)}, u32[]{:S(2)}, u32[]{:S(2)}) collective-permute-start(bf16[1024,1024]{1,0:T(8,128)(2,1)} %collective-permute-done.4), channel_id=1, source_target_pairs={{0,2},{2,4},{4,6},{6,8},{8,10},{10,12},{12,14},{14,0},{1,3},{3,5},... | collective-permute-start | bytes 6291464 | tf_op jit(solution)/shard_map/ppermute | solution.py:112
  174.1 29.7 %copy-start.11 = (f32[8192]{0:T(1024)S(1)}, f32[8192]{0:T(1024)}, u32[]{:S(2)}) copy-start(f32[8192]{0:T(1024)} %param.15) | copy-start | bytes 98308
  197.5 27.6 %collective-permute-start.6 = (bf16[1024,1024]{1,0:T(8,128)(2,1)}, bf16[1024,1024]{1,0:T(8,128)(2,1)}, u32[]{:S(2)}, u32[]{:S(2)}) collective-permute-start(bf16[1024,1024]{1,0:T(8,128)(2,1)} %collective-permute-done.5), channel_id=1, source_target_pairs={{0,2},{2,4},{4,6},{6,8},{8,10},{10,12},{12,14},{14,0},{1,3},{3,5},... | collective-permute-start | bytes 6291464 | tf_op jit(solution)/shard_map/ppermute | solution.py:112
  203.7 6.6 %copy-start.9 = (f32[128]{0:T(128)S(1)}, f32[128]{0:T(128)}, u32[]{:S(2)}) copy-start(f32[128]{0:T(128)} %param.21) | copy-start | bytes 1540
  203.7 6.6 %copy-start.10 = (f32[128]{0:T(128)S(1)}, f32[128]{0:T(128)}, u32[]{:S(2)}) copy-start(f32[128]{0:T(128)} %param.20) | copy-start | bytes 1540
  228.1 6.4 %copy-start.4 = (bf16[1024,1024]{1,0:T(8,128)(2,1)S(1)}, bf16[1024,1024]{1,0:T(8,128)(2,1)}, u32[]{:S(2)}) copy-start(bf16[1024,1024]{1,0:T(8,128)(2,1)} %copy-done.3) | copy-start | bytes 6291460
  231.3 4.7 copy-start.2
  260.7 5.1 copy-start.7
  265.8 9.6 %copy-start.12 = (s32[16]{0:T(128)S(1)}, s32[16]{0:T(128)}, u32[]{:S(2)}) copy-start(s32[16]{0:T(128)} %param.22) | copy-start | bytes 196
  265.8 9.6 %copy-start.13 = (s32[16]{0:T(128)S(1)}, s32[16]{0:T(128)}, u32[]{:S(2)}) copy-start(s32[16]{0:T(128)} %param.23) | copy-start | bytes 196
  274.1 7.6 %copy-start.14 = (f32[1024]{0:T(1024)S(1)}, f32[1024]{0:T(1024)}, u32[]{:S(2)}) copy-start(f32[1024]{0:T(1024)} %param.19) | copy-start | bytes 12292
  275.0 67.7 %all-gather.10.cloned.1.call-start = ((), (), s32[]{:S(2)}) async-start(), calls=%async_computation.2 | async-start | bytes 1802240 | tf_op jit(solution)/shard_map/all_gather | solution.py:159
  342.8 207.1 %copy-start.8 = (pred[1024]{0:T(1024)(128)(4,1)S(1)}, pred[1024]{0:T(1024)(128)(4,1)}, u32[]{:S(2)}) copy-start(pred[1024]{0:T(1024)(128)(4,1)} %fusion.85) | copy-start | bytes 3076
  416.5 28.9 %copy-start.5 = (f32[1024,1,8]{0,2,1:T(8,128)S(1)}, f32[1024,1,8]{0,2,1:T(8,128)}, u32[]{:S(2)}) copy-start(f32[1024,1,8]{0,2,1:T(8,128)} %get-tuple-element.533) | copy-start | bytes 98308 | tf_op jit(solution)/shard_map/while
  445.4 0.6 copy-start.6
  520.4 28.9 %copy-start.5 = (f32[1024,1,8]{0,2,1:T(8,128)S(1)}, f32[1024,1,8]{0,2,1:T(8,128)}, u32[]{:S(2)}) copy-start(f32[1024,1,8]{0,2,1:T(8,128)} %get-tuple-element.533) | copy-start | bytes 98308 | tf_op jit(solution)/shard_map/while
  549.2 0.6 copy-start.6
Sparse Core Ops, SparseCore 0:
  8.9 35.8 all-gather.5
  46.3 33.0 all-gather.7
  80.9 198.8 all-gather.11
  281.5 29.7 all-gather.13
  313.0 29.7 all-gather.9
